TPU v7x, 128 devices: a whole 4x4x4 slice. The times are simulated.
128 devices in a mesh: sub: 16 (over z, x), grp: 8 (over y, core).
Axes of the slice: x: 4, y: 4, z: 4, core: 2. Of those that a mesh axis runs over, the one named last changes fastest.
Arguments:
- rhs: float32 [8, 64, 256, 256], P('grp', 'sub')
- counts: int32 [8, 64], P('grp', 'sub'), may hold values from 64 to 256, as said below
- solve_panel: bfloat16 [8, 64, 512, 512], P('grp', 'sub'), as said below
- dirichlet_panel: bfloat16 [8, 64, 512, 512], P('grp', 'sub'), as said below
- coupling: float32 [8, 64, 32, 512], P('grp', 'sub'), may hold values from -0.25 to 0.25
- corner_map: int32 [8, 64, 32], P('grp', 'sub'), may hold values from 0 to 2047
- coarse_inverse: float32 [16, 2048, 2048], P('sub', 'grp'), as said below
Outputs:
- multipliers: float32 [8, 64, 256, 256], P('grp', 'sub')
- residual: float32 [8, 64, 256, 256], P('grp', 'sub')
Inputs may be any that keep to these rules, and one draw needn't show every extreme that they name: `counts`: some pair has all 256 unknowns constrained. `solve_panel`: each panel is symmetric positive definite. `dirichlet_panel`: each panel is symmetric positive definite. `coarse_inverse`: each slab's matrix is symmetric positive definite.
All inputs are finite; a program needn't handle non-finite values.
Results may differ from a plain program's by a relative error of at most 0.0003.
Values sent between devices are 32-bit elements; how exact they have to be, the bound alone decides.
A program may use at most 128 MiB of HBM per device.

v0:
```python
import jax
import jax.numpy as jnp
from jax import lax
from jax.sharding import PartitionSpec as P

ITERS = 3
HIGH = lax.Precision.HIGHEST


def passed_along(block, axis, distance):
    devices = range(lax.axis_size(axis))
    route = [(i - distance, i) for i in devices if i - distance in devices]
    return lax.ppermute(block, axis, route)


def spread_faces(values):
    previous = passed_along(values[:, -1:], "sub", 1)
    prior = jnp.concatenate([previous, values[:, :-1]], axis=1)
    return jnp.concatenate([-prior, values], axis=3)


def face_jump(result, live_mask):
    width = result.shape[3] // 2
    following = passed_along(result[:, :1, :, :width], "sub", -1)
    next_left = jnp.concatenate([result[:, 1:, :, :width], following], axis=1)
    return live_mask * (result[..., width:] - next_left)


def panel_apply(panel, face_vals):
    return jnp.einsum(
        "gsrp,gsqp->gsrq", face_vals, panel, precision=HIGH, preferred_element_type=jnp.float32
    )


def inner(first, second):
    return jnp.sum(first * second, axis=(0, 1, 3))


def expand(scalars):
    return scalars[None, None, :, None]


def residual_sum(resid, precond):
    return lax.psum(inner(resid, precond), ("sub", "grp"))


def local(rhs, counts, solve_panel, dirichlet_panel, coupling, corner_map, coarse_inverse):
    local_subs = rhs.shape[1]
    width = rhs.shape[3]
    size = coarse_inverse.shape[2]
    last_device = lax.axis_index("sub") == lax.axis_size("sub") - 1
    slots = jnp.arange(local_subs, dtype=jnp.int32)
    positions = jnp.arange(width, dtype=jnp.int32)
    not_last = jnp.logical_not(last_device & (slots == local_subs - 1))
    live = (positions[None, None, :] < counts[:, :, None]) & not_last[None, :, None]
    live_mask = live.astype(jnp.float32)[:, :, None, :]
    corner_onehot = (corner_map[0][..., None] == jnp.arange(size, dtype=jnp.int32)).astype(
        jnp.float32
    )

    def precondition(values):
        return 0.25 * face_jump(panel_apply(dirichlet_panel, spread_faces(values)), live_mask)

    multipliers = jnp.zeros_like(rhs)
    residual = live_mask * rhs
    precond = precondition(residual)
    direction = precond
    rz_now = residual_sum(residual, precond)
    for step in range(ITERS):
        apply_face_vals = spread_faces(direction)
        corner_vals = jnp.einsum("srp,skp->srk", apply_face_vals[0], coupling[0], precision=HIGH)
        owned_totals = lax.psum_scatter(
            jnp.einsum("skn,srk->nr", corner_onehot, corner_vals, precision=HIGH),
            "grp",
            scatter_dimension=0,
            tiled=True,
        )
        partial_solved = jnp.einsum("mn,mr->nr", coarse_inverse[0], owned_totals, precision=HIGH)
        solved = lax.psum(partial_solved, "grp")
        back = jnp.einsum("skn,nr->srk", corner_onehot, solved, precision=HIGH)
        result = (
            panel_apply(solve_panel, apply_face_vals)
            + jnp.einsum("srk,skp->srp", back, coupling[0], precision=HIGH)[None]
        )
        image = face_jump(result, live_mask)
        alpha = rz_now / lax.psum(inner(direction, image), ("sub", "grp"))
        multipliers = multipliers + expand(alpha) * direction
        residual = residual - expand(alpha) * image
        if step + 1 < ITERS:
            precond = precondition(residual)
            rz_next = residual_sum(residual, precond)
            direction = precond + expand(rz_next / rz_now) * direction
            rz_now = rz_next
    return (multipliers, residual)


def solution(mesh):
    return jax.shard_map(
        local,
        mesh=mesh,
        in_specs=(
            P("grp", "sub", None, None),
            P("grp", "sub"),
            P("grp", "sub", None, None),
            P("grp", "sub", None, None),
            P("grp", "sub", None, None),
            P("grp", "sub", None),
            P("sub", "grp", None),
        ),
        out_specs=(P("grp", "sub", None, None), P("grp", "sub", None, None)),
        check_vma=False,
    )
```

profile of v0, /device:TPU:1, one launch (start us, length us, event | category | flops | bytes accessed | tf_op | source)
XLA Modules:
  0.0 832.8 jit_solution(642383770802080915)
XLA Ops:
  7.2 0.9 fusion.82
  8.1 1.3 broadcast_multiply_fusion.1
  9.4 4.0 collective-permute-start
  13.5 4.9 collective-permute-done
  18.5 1.8 fusion.42
  20.3 1.3 collective-permute-start.1
  21.7 7.8 collective-permute-done.1
  29.7 3.2 collective-permute-start.2
  33.1 3.2 collective-permute-done.2
  36.4 1.9 fusion.29
  38.3 3.7 convolution_bitcast_fusion.2
  42.0 38.6 %reduce-scatter.4.cloned.1.call-done = f32[256,256]{1,0:T(8,128)} async-done(((f32[2048,256]{1,0:T(8,128)}), f32[256,256]{1,0:T(8,128)}) %reduce-scatter.4.cloned.1.call-update) | async-done | bytes 262160 | tf_op jit(solution)/shard_map/reduce_scatter | solution.py:72
  80.6 4.9 convolution_bitcast_fusion.5
  85.8 65.4 %all-reduce.5.cloned.1.call-done = f32[2048,256]{0,1:T(8,128)} async-done(((f32[2048,256]{0,1:T(8,128)}), f32[2048,256]{0,1:T(8,128)}) %all-reduce.5.cloned.1.call-update) | async-done | bytes 2097168 | tf_op jit(solution)/shard_map/psum | solution.py:79
  151.2 3.1 fusion.45
  154.3 1.8 fusion.78
  156.2 1.8 add_bitcast_fusion.2
  158.1 1.6 collective-permute-start.3
  159.7 5.7 collective-permute-done.3
  166.2 70.6 %all-reduce = (f32[256]{0:T(256)S(1)}, f32[256]{0:T(256)S(1)}) all-reduce(f32[256]{0:T(256)S(1)} %get-tuple-element.3, f32[256]{0:T(256)S(1)} %get-tuple-element.2), channel_id=1, replica_groups=mesh['sub'=16,'grp'=8] {'sub','grp'}, use_global_device_ids=true, to_apply=%region_1.0 | all-reduce | flops 512 | bytes 4096 | tf_op jit(solution)/shard_map/psum | solution.py:44
  236.8 2.1 multiply_subtract_fusion.2
  238.9 2.5 collective-permute-start.4
  241.4 4.6 collective-permute-done.4
  246.1 1.8 fusion.39
  248.0 1.3 collective-permute-start.5
  249.4 7.5 collective-permute-done.5
  258.0 67.7 %psum.66 = f32[256]{0:T(256)S(1)} all-reduce(f32[256]{0:T(256)S(1)} %multiply_reduce_fusion.3), channel_id=1, replica_groups=mesh['sub'=16,'grp'=8] {'sub','grp'}, use_global_device_ids=true, to_apply=%region_7.0 | all-reduce | flops 256 | bytes 2048 | tf_op jit(solution)/shard_map/psum | solution.py:44
  325.7 2.1 multiply_add_fusion.2
  327.8 2.6 collective-permute-start.6
  330.5 4.6 collective-permute-done.6
  335.1 1.0 copy-done.20
  336.1 1.9 fusion.28
  338.0 3.7 convolution_bitcast_fusion.1
  341.7 32.0 %reduce-scatter.6.cloned.1.call-done = f32[256,256]{1,0:T(8,128)} async-done(((f32[2048,256]{1,0:T(8,128)}), f32[256,256]{1,0:T(8,128)}) %reduce-scatter.6.cloned.1.call-update) | async-done | bytes 262160 | tf_op jit(solution)/shard_map/reduce_scatter | solution.py:72
  373.7 4.9 convolution_bitcast_fusion.4
  378.7 65.6 %all-reduce.7.cloned.1.call-done = f32[2048,256]{0,1:T(8,128)} async-done(((f32[2048,256]{0,1:T(8,128)}), f32[2048,256]{0,1:T(8,128)}) %all-reduce.7.cloned.1.call-update) | async-done | bytes 2097168 | tf_op jit(solution)/shard_map/psum | solution.py:79
  444.4 3.1 fusion.48
  447.5 1.8 fusion.75
  449.3 1.8 add_bitcast_fusion.1
  451.2 1.3 collective-permute-start.7
  452.6 5.7 collective-permute-done.7
  459.4 71.1 %psum.68 = f32[256]{0:T(256)S(1)} all-reduce(f32[256]{0:T(256)S(1)} %multiply_reduce_fusion.2), channel_id=1, replica_groups=mesh['sub'=16,'grp'=8] {'sub','grp'}, use_global_device_ids=true, to_apply=%region_11.0 | all-reduce | flops 256 | bytes 2048 | tf_op jit(solution)/shard_map/psum | solution.py:86
  530.5 2.1 multiply_subtract_fusion.1
  532.6 2.5 collective-permute-start.8
  535.1 4.6 collective-permute-done.8
  539.8 1.8 fusion.36
  541.6 1.3 collective-permute-start.9
  543.0 7.5 collective-permute-done.9
  551.6 67.7 %psum.69 = f32[256]{0:T(256)S(1)} all-reduce(f32[256]{0:T(256)S(1)} %multiply_reduce_fusion.1), channel_id=1, replica_groups=mesh['sub'=16,'grp'=8] {'sub','grp'}, use_global_device_ids=true, to_apply=%region_13.0 | all-reduce | flops 256 | bytes 2048 | tf_op jit(solution)/shard_map/psum | solution.py:44
  619.3 1.8 multiply_add_fusion.1
  621.1 2.4 collective-permute-start.10
  623.6 4.8 collective-permute-done.10
  628.4 1.9 fusion.27
  630.3 3.7 convolution_bitcast_fusion
  634.3 31.8 %reduce-scatter.8.cloned.1.call-done = f32[256,256]{1,0:T(8,128)} async-done(((f32[2048,256]{1,0:T(8,128)}), f32[256,256]{1,0:T(8,128)}) %reduce-scatter.8.cloned.1.call-update) | async-done | bytes 262160 | tf_op jit(solution)/shard_map/reduce_scatter | solution.py:72
  666.1 4.9 convolution_bitcast_fusion.3
  671.0 65.7 %all-reduce.9.cloned.1.call-done = f32[2048,256]{0,1:T(8,128)} async-done(((f32[2048,256]{0,1:T(8,128)}), f32[2048,256]{0,1:T(8,128)}) %all-reduce.9.cloned.1.call-update) | async-done | bytes 2097168 | tf_op jit(solution)/shard_map/psum | solution.py:79
  736.7 3.1 fusion.51
  739.8 1.8 fusion.72
  741.7 1.8 add_bitcast_fusion
  743.6 1.3 collective-permute-start.11
  744.9 5.7 collective-permute-done.11
  750.9 70.7 %psum.71 = f32[256]{0:T(256)S(1)} all-reduce(f32[256]{0:T(256)S(1)} %multiply_reduce_fusion), channel_id=1, replica_groups=mesh['sub'=16,'grp'=8] {'sub','grp'}, use_global_device_ids=true, to_apply=%region_17.0 | all-reduce | flops 256 | bytes 2048 | tf_op jit(solution)/shard_map/psum | solution.py:86
  821.6 4.1 multiply_subtract_fusion
  (121 shorter events, 6.5 us)
Async XLA Ops:
  7.2 11.3 %copy-start = (bf16[1,4,512,512]{3,2,1,0:T(8,128)(2,1)S(1)}, bf16[1,4,512,512]{3,2,1,0:T(8,128)(2,1)}, u32[]{:S(2)}) copy-start(bf16[1,4,512,512]{3,2,1,0:T(8,128)(2,1)} %param.10) | copy-start | bytes 6291460
  7.2 73.4 %reduce-scatter.4.cloned.1.call-start = ((), (), s32[]{:S(2)}) async-start(), calls=%async_computation.3 | async-start | bytes 2359296 | tf_op jit(solution)/shard_map/reduce_scatter | solution.py:72
  9.4 8.9 %collective-permute-start = (f32[1,1,256,256]{3,2,1,0:T(8,128)S(1)}, f32[1,1,256,256]{3,2,1,0:T(8,128)S(1)}, u32[]{:S(2)}, u32[]{:S(2)}) collective-permute-start(f32[1,1,256,256]{3,2,1,0:T(8,128)S(1)} %slice.120), channel_id=1, source_target_pairs={{0,8},{8,16},{16,24},{24,32},{32,40},{40,48},{48,56},{56,64},{64,7... | collective-permute-start | bytes 786440 | tf_op jit(solution)/shard_map/ppermute | solution.py:13
  20.3 9.2 %collective-permute-start.1 = (f32[1,1,256,256]{3,2,1,0:T(8,128)S(1)}, f32[1,1,256,256]{3,2,1,0:T(8,128)S(1)}, u32[]{:S(2)}, u32[]{:S(2)}) collective-permute-start(f32[1,1,256,256]{3,2,1,0:T(8,128)S(1)} %slice.124), channel_id=1, source_target_pairs={{8,0},{16,8},{24,16},{32,24},{40,32},{48,40},{56,48},{64,56},{72,6... | collective-permute-start | bytes 786440 | tf_op jit(solution)/shard_map/ppermute | solution.py:13
  29.7 6.7 copy-start.9
  29.7 135.8 %copy-start.8 = (f32[1,4,256,256]{3,2,1,0:T(8,128)}, f32[1,4,256,256]{3,2,1,0:T(8,128)S(1)}, u32[]{:S(2)}) copy-start(f32[1,4,256,256]{3,2,1,0:T(8,128)S(1)} %get-tuple-element.9) | copy-start | bytes 3145732
  29.7 6.6 copy-start.17
  29.7 6.5 collective-permute-start.2
  33.0 5.2 copy-start.33
  36.4 1.9 copy-start.18
  42.0 109.2 %all-reduce.5.cloned.1.call-start = ((), (), s32[]{:S(2)}) async-start(), calls=%async_computation.4 | async-start | bytes 4194304 | tf_op jit(solution)/shard_map/psum | solution.py:79
  85.5 288.2 %reduce-scatter.6.cloned.1.call-start = ((), (), s32[]{:S(2)}) async-start(), calls=%async_computation.5 | async-start | bytes 2359296 | tf_op jit(solution)/shard_map/reduce_scatter | solution.py:72
  151.2 5.0 copy-start.5
  151.2 5.0 copy-start.10
  151.2 5.0 copy-start.19
  158.0 7.9 copy-start.14
  158.0 7.4 copy-start.16
  158.1 7.4 collective-permute-start.3
  159.7 6.3 copy-start.25
  165.5 0.7 copy-start.29
  238.9 18.0 %copy-start.4 = (f32[1,4,256,256]{3,2,1,0:T(8,128)}, f32[1,4,256,256]{3,2,1,0:T(8,128)S(1)}, u32[]{:S(2)}) copy-start(f32[1,4,256,256]{3,2,1,0:T(8,128)S(1)} %multiply_subtract_fusion.2) | copy-start | bytes 3145732
  238.9 7.1 collective-permute-start.4
  248.0 8.9 %copy-start.11 = (f32[1,4,256,512]{3,2,1,0:T(8,128)}, f32[1,4,256,512]{3,2,1,0:T(8,128)S(1)}, u32[]{:S(2)}) copy-start(f32[1,4,256,512]{3,2,1,0:T(8,128)S(1)} %fusion.39) | copy-start | bytes 6291460
  248.0 8.9 %collective-permute-start.5 = (f32[1,1,256,256]{3,2,1,0:T(8,128)S(1)}, f32[1,1,256,256]{3,2,1,0:T(8,128)S(1)}, u32[]{:S(2)}, u32[]{:S(2)}) collective-permute-start(f32[1,1,256,256]{3,2,1,0:T(8,128)S(1)} %slice.134), channel_id=1, source_target_pairs={{8,0},{16,8},{24,16},{32,24},{40,32},{48,40},{56,48},{64,56},{72,6... | collective-permute-start | bytes 786440 | tf_op jit(solution)/shard_map/ppermute | solution.py:13
  249.4 7.5 copy-start.27
  256.9 0.7 copy-start.31
  327.8 7.2 collective-permute-start.6
  335.1 1.0 copy-start.20
  341.7 102.7 %all-reduce.7.cloned.1.call-start = ((), (), s32[]{:S(2)}) async-start(), calls=%async_computation.6 | async-start | bytes 4194304 | tf_op jit(solution)/shard_map/psum | solution.py:79
  378.7 287.4 %reduce-scatter.8.cloned.1.call-start = ((), (), s32[]{:S(2)}) async-start(), calls=%async_computation.7 | async-start | bytes 2359296 | tf_op jit(solution)/shard_map/reduce_scatter | solution.py:72
  444.4 5.0 copy-start.6
  444.4 5.0 copy-start.21
  451.2 7.2 copy-start.15
  451.2 7.1 collective-permute-start.7
  452.6 5.7 copy-start.26
  458.3 0.7 copy-start.30
  532.5 18.0 %copy-start.3 = (f32[1,4,256,256]{3,2,1,0:T(8,128)}, f32[1,4,256,256]{3,2,1,0:T(8,128)S(1)}, u32[]{:S(2)}) copy-start(f32[1,4,256,256]{3,2,1,0:T(8,128)S(1)} %multiply_subtract_fusion.1) | copy-start | bytes 3145732
  532.6 7.1 collective-permute-start.8
  541.6 8.9 %copy-start.12 = (f32[1,4,256,512]{3,2,1,0:T(8,128)}, f32[1,4,256,512]{3,2,1,0:T(8,128)S(1)}, u32[]{:S(2)}) copy-start(f32[1,4,256,512]{3,2,1,0:T(8,128)S(1)} %fusion.36) | copy-start | bytes 6291460
  541.6 8.9 %collective-permute-start.9 = (f32[1,1,256,256]{3,2,1,0:T(8,128)S(1)}, f32[1,1,256,256]{3,2,1,0:T(8,128)S(1)}, u32[]{:S(2)}, u32[]{:S(2)}) collective-permute-start(f32[1,1,256,256]{3,2,1,0:T(8,128)S(1)} %slice.144), channel_id=1, source_target_pairs={{8,0},{16,8},{24,16},{32,24},{40,32},{48,40},{56,48},{64,56},{72,6... | collective-permute-start | bytes 786440 | tf_op jit(solution)/shard_map/ppermute | solution.py:13
  543.0 7.5 copy-start.28
  550.5 0.7 copy-start.32
  621.1 7.4 copy-start.1
  621.1 7.2 collective-permute-start.10
  628.4 1.9 copy-start.22
  634.1 102.6 %all-reduce.9.cloned.1.call-start = ((), (), s32[]{:S(2)}) async-start(), calls=%async_computation.8 | async-start | bytes 4194304 | tf_op jit(solution)/shard_map/psum | solution.py:79
  736.7 5.0 copy-start.2
  736.7 5.0 copy-start.7
  736.7 5.0 copy-start.23
  743.5 7.2 copy-start.13
  743.6 7.1 collective-permute-start.11
  744.9 5.7 copy-start.24
Sparse Core Ops, SparseCore 0:
  42.1 38.4 reduce-scatter.3
  85.7 65.4 all-reduce.4
  341.8 31.8 reduce-scatter.5
  378.8 65.5 all-reduce.6
  634.2 31.8 reduce-scatter.7
  671.1 65.4 all-reduce.8
where the time goes:
time: 841 us; the launch traced here: 833 us
  waiting for transfers between devices  366 us (44%)
  blocking collectives  348 us (41%)
  matrix products  57.2 us (7%)
  starting transfers between devices  25.7 us (3%)
  other arithmetic  16.7 us (2%)
  between operations  15.2 us (2%)
    psum x3, blocking collectives, residual_sum(): return lax.psum(inner(resid, precond), ('sub', 'grp'))  206 us
    psum x3, waiting for transfers between devices, local(): solved = lax.psum(partial_solved, 'grp')  197 us
    psum x2, blocking collectives, local(): alpha = rz_now / lax.psum(inner(direction, image), ('sub', 'grp'))  142 us
    reduce_scatter x3, waiting for transfers between devices, local(): lax.psum_scatter(jnp.einsum('skn,srk->nr', corner_onehot, corner_vals, pr...  102 us
    ppermute x12, waiting for transfers between devices, passed_along(): return lax.ppermute(block, axis, route)  66.6 us
    ppermute x12, starting transfers between devices, passed_along(): return lax.ppermute(block, axis, route)  25.1 us
  transfers between devices with their start and end apart: 18, of which 18 were waited for; matrix products, arithmetic and copies ran while one was open for 0% of the time, Pallas kernels for 0%

commit v1 on v0

--- a/solution.py
+++ b/solution.py
@@ -76,7 +76,9 @@
             tiled=True,
         )
         partial_solved = jnp.einsum("mn,mr->nr", coarse_inverse[0], owned_totals, precision=HIGH)
-        solved = lax.psum(partial_solved, "grp")
+        solved = partial_solved
+        for hop in (1, 2, 4):
+            solved = solved + lax.ppermute(solved, "grp", [(dev, dev ^ hop) for dev in range(8)])
         back = jnp.einsum("skn,nr->srk", corner_onehot, solved, precision=HIGH)
         result = (
             panel_apply(solve_panel, apply_face_vals)

time: 841 us -> 936 us (1.11)
  waiting for transfers between devices: 366 us -> 463 us
  starting transfers between devices: 25.7 us -> 39.3 us
  blocking collectives: 348 us -> 338 us
    ppermute x0 -> x9, waiting for transfers between devices: none -> 293 us  [local(): lax.ppermute(solved, 'grp', [(dev, dev ^ hop) for dev in range(8)])]
    psum x3 -> x0, waiting for transfers between devices: 197 us -> none  [local(): solved = lax.psum(partial_solved, 'grp')]
    ppermute x0 -> x9, starting transfers between devices: none -> 13.6 us  [local(): lax.ppermute(solved, 'grp', [(dev, dev ^ hop) for dev in range(8)])]
  transfers between devices with their start and end apart: 18 -> 24, of which waited for: 18 -> 24; matrix products, arithmetic and copies ran while one was open for 0% -> 0% of each run, Pallas kernels for 0% -> 0%
where the time goes in v1:
time: 936 us; the launch traced here: 927 us
  waiting for transfers between devices  463 us (49%)
  blocking collectives  338 us (36%)
  matrix products  48.2 us (5%)
  starting transfers between devices  39.3 us (4%)
  other arithmetic  18.6 us (2%)
  between operations  14.9 us (2%)
    ppermute x9, waiting for transfers between devices, local(): lax.ppermute(solved, 'grp', [(dev, dev ^ hop) for dev in range(8)])  293 us
    psum x3, blocking collectives, residual_sum(): return lax.psum(inner(resid, precond), ('sub', 'grp'))  202 us
    psum x2, blocking collectives, local(): alpha = rz_now / lax.psum(inner(direction, image), ('sub', 'grp'))  136 us
    reduce_scatter x3, waiting for transfers between devices, local(): lax.psum_scatter(jnp.einsum('skn,srk->nr', corner_onehot, corner_vals, pr...  102 us
    ppermute x12, waiting for transfers between devices, passed_along(): return lax.ppermute(block, axis, route)  68.3 us
    ppermute x12, starting transfers between devices, passed_along(): return lax.ppermute(block, axis, route)  25.5 us
  transfers between devices with their start and end apart: 24, of which 24 were waited for; matrix products, arithmetic and copies ran while one was open for 0% of the time, Pallas kernels for 0%

profile of v1, /device:TPU:1, one launch (start us, length us, event | category | flops | bytes accessed | tf_op | source)
XLA Modules:
  0.0 926.9 jit_solution(7916336470234231459)
XLA Ops:
  9.4 4.0 collective-permute-start
  13.5 4.9 collective-permute-done
  18.5 1.8 fusion.45
  21.7 7.8 collective-permute-done.1
  29.7 3.2 collective-permute-start.2
  33.1 3.2 collective-permute-done.2
  36.4 1.9 fusion.32
  38.3 3.7 convolution_bitcast_fusion.2
  42.0 38.6 %reduce-scatter.4.cloned.1.call-done = f32[256,256]{1,0:T(8,128)} async-done(((f32[2048,256]{1,0:T(8,128)}), f32[256,256]{1,0:T(8,128)}) %reduce-scatter.4.cloned.1.call-update) | async-done | bytes 262160 | tf_op jit(solution)/shard_map/reduce_scatter | solution.py:72
  80.6 3.6 convolution_bitcast_fusion.5
  84.2 3.7 collective-permute-start.3
  87.9 3.8 collective-permute-done.3
  92.1 46.8 %collective-permute-done.4 = f32[2048,256]{0,1:T(8,128)S(1)} collective-permute-done((f32[2048,256]{0,1:T(8,128)S(1)}, f32[2048,256]{0,1:T(8,128)S(1)}, u32[]{:S(2)}, u32[]{:S(2)}) %collective-permute-start.4) | collective-permute-done | bytes 2097184 | tf_op jit(solution)/shard_map/ppermute | solution.py:81
  139.9 46.9 %collective-permute-done.5 = f32[2048,256]{0,1:T(8,128)S(1)} collective-permute-done((f32[2048,256]{0,1:T(8,128)S(1)}, f32[2048,256]{0,1:T(8,128)S(1)}, u32[]{:S(2)}, u32[]{:S(2)}) %collective-permute-start.5) | collective-permute-done | bytes 2097184 | tf_op jit(solution)/shard_map/ppermute | solution.py:81
  186.9 1.5 fusion.48
  188.4 1.8 fusion.81
  190.2 1.8 add_bitcast_fusion.2
  192.1 1.6 collective-permute-start.6
  193.8 6.2 collective-permute-done.6
  200.7 67.7 %all-reduce = (f32[256]{0:T(256)S(1)}, f32[256]{0:T(256)S(1)}) all-reduce(f32[256]{0:T(256)S(1)} %get-tuple-element.3, f32[256]{0:T(256)S(1)} %get-tuple-element.2), channel_id=1, replica_groups=mesh['sub'=16,'grp'=8] {'sub','grp'}, use_global_device_ids=true, to_apply=%region_1.0 | all-reduce | flops 512 | bytes 4096 | tf_op jit(solution)/shard_map/psum | solution.py:44
  268.4 2.1 multiply_subtract_fusion.2
  270.6 2.6 collective-permute-start.7
  273.3 4.7 collective-permute-done.7
  278.1 1.8 fusion.42
  281.4 7.6 collective-permute-done.8
  290.1 67.3 %psum.44 = f32[256]{0:T(256)S(1)} all-reduce(f32[256]{0:T(256)S(1)} %multiply_reduce_fusion.3), channel_id=1, replica_groups=mesh['sub'=16,'grp'=8] {'sub','grp'}, use_global_device_ids=true, to_apply=%region_6.0 | all-reduce | flops 256 | bytes 2048 | tf_op jit(solution)/shard_map/psum | solution.py:44
  357.4 2.1 multiply_add_fusion.2
  359.5 2.6 collective-permute-start.9
  362.1 4.5 collective-permute-done.9
  367.7 1.9 fusion.31
  369.6 3.7 convolution_bitcast_fusion.1
  373.3 31.8 %reduce-scatter.6.cloned.1.call-done = f32[256,256]{1,0:T(8,128)} async-done(((f32[2048,256]{1,0:T(8,128)}), f32[256,256]{1,0:T(8,128)}) %reduce-scatter.6.cloned.1.call-update) | async-done | bytes 262160 | tf_op jit(solution)/shard_map/reduce_scatter | solution.py:72
  405.2 3.6 convolution_bitcast_fusion.4
  408.8 3.7 collective-permute-start.10
  412.4 3.8 collective-permute-done.10
  416.7 46.8 %collective-permute-done.11 = f32[2048,256]{0,1:T(8,128)S(1)} collective-permute-done((f32[2048,256]{0,1:T(8,128)S(1)}, f32[2048,256]{0,1:T(8,128)S(1)}, u32[]{:S(2)}, u32[]{:S(2)}) %collective-permute-start.11) | collective-permute-done | bytes 2097184 | tf_op jit(solution)/shard_map/ppermute | solution.py:81
  464.8 46.9 %collective-permute-done.12 = f32[2048,256]{0,1:T(8,128)S(1)} collective-permute-done((f32[2048,256]{0,1:T(8,128)S(1)}, f32[2048,256]{0,1:T(8,128)S(1)}, u32[]{:S(2)}, u32[]{:S(2)}) %collective-permute-start.12) | collective-permute-done | bytes 2097184 | tf_op jit(solution)/shard_map/ppermute | solution.py:81
  511.7 1.4 fusion.51
  513.2 1.8 fusion.78
  515.1 1.8 add_bitcast_fusion.1
  518.3 6.2 collective-permute-done.13
  525.6 67.9 %psum.45 = f32[256]{0:T(256)S(1)} all-reduce(f32[256]{0:T(256)S(1)} %multiply_reduce_fusion.2), channel_id=1, replica_groups=mesh['sub'=16,'grp'=8] {'sub','grp'}, use_global_device_ids=true, to_apply=%region_9.0 | all-reduce | flops 256 | bytes 2048 | tf_op jit(solution)/shard_map/psum | solution.py:88
  593.5 2.1 multiply_subtract_fusion.1
  595.6 2.6 collective-permute-start.14
  598.3 4.8 collective-permute-done.14
  603.1 1.8 fusion.39
  606.4 7.7 collective-permute-done.15
  615.1 67.2 %psum.46 = f32[256]{0:T(256)S(1)} all-reduce(f32[256]{0:T(256)S(1)} %multiply_reduce_fusion.1), channel_id=1, replica_groups=mesh['sub'=16,'grp'=8] {'sub','grp'}, use_global_device_ids=true, to_apply=%region_11.0 | all-reduce | flops 256 | bytes 2048 | tf_op jit(solution)/shard_map/psum | solution.py:44
  682.3 1.8 multiply_add_fusion.1
  684.1 2.5 collective-permute-start.16
  686.7 4.6 collective-permute-done.16
  691.4 1.9 fusion.30
  693.3 3.7 convolution_bitcast_fusion
  697.0 32.0 %reduce-scatter.8.cloned.1.call-done = f32[256,256]{1,0:T(8,128)} async-done(((f32[2048,256]{1,0:T(8,128)}), f32[256,256]{1,0:T(8,128)}) %reduce-scatter.8.cloned.1.call-update) | async-done | bytes 262160 | tf_op jit(solution)/shard_map/reduce_scatter | solution.py:72
  729.0 3.6 convolution_bitcast_fusion.3
  732.6 3.7 collective-permute-start.17
  736.3 3.8 collective-permute-done.17
  740.5 46.8 %collective-permute-done.18 = f32[2048,256]{0,1:T(8,128)S(1)} collective-permute-done((f32[2048,256]{0,1:T(8,128)S(1)}, f32[2048,256]{0,1:T(8,128)S(1)}, u32[]{:S(2)}, u32[]{:S(2)}) %collective-permute-start.18) | collective-permute-done | bytes 2097184 | tf_op jit(solution)/shard_map/ppermute | solution.py:81
  788.3 46.9 %collective-permute-done.19 = f32[2048,256]{0,1:T(8,128)S(1)} collective-permute-done((f32[2048,256]{0,1:T(8,128)S(1)}, f32[2048,256]{0,1:T(8,128)S(1)}, u32[]{:S(2)}, u32[]{:S(2)}) %collective-permute-start.19) | collective-permute-done | bytes 2097184 | tf_op jit(solution)/shard_map/ppermute | solution.py:81
  836.7 1.8 fusion.75
  838.5 1.8 add_bitcast_fusion
  841.8 6.2 collective-permute-done.20
  848.2 67.8 %psum.47 = f32[256]{0:T(256)S(1)} all-reduce(f32[256]{0:T(256)S(1)} %multiply_reduce_fusion), channel_id=1, replica_groups=mesh['sub'=16,'grp'=8] {'sub','grp'}, use_global_device_ids=true, to_apply=%region_14.0 | all-reduce | flops 256 | bytes 2048 | tf_op jit(solution)/shard_map/psum | solution.py:88
  916.1 4.1 multiply_subtract_fusion
  (136 shorter events, 21.5 us)
Async XLA Ops:
  7.2 11.3 %copy-start = (bf16[1,4,512,512]{3,2,1,0:T(8,128)(2,1)S(1)}, bf16[1,4,512,512]{3,2,1,0:T(8,128)(2,1)}, u32[]{:S(2)}) copy-start(bf16[1,4,512,512]{3,2,1,0:T(8,128)(2,1)} %param.10) | copy-start | bytes 6291460
  7.2 73.4 %reduce-scatter.4.cloned.1.call-start = ((), (), s32[]{:S(2)}) async-start(), calls=%async_computation.3 | async-start | bytes 2359296 | tf_op jit(solution)/shard_map/reduce_scatter | solution.py:72
  9.4 8.9 collective-permute-start
  20.3 9.2 collective-permute-start.1
  29.7 6.7 copy-start.9
  29.7 170.3 %copy-start.8 = (f32[1,4,256,256]{3,2,1,0:T(8,128)}, f32[1,4,256,256]{3,2,1,0:T(8,128)S(1)}, u32[]{:S(2)}) copy-start(f32[1,4,256,256]{3,2,1,0:T(8,128)S(1)} %get-tuple-element.9) | copy-start | bytes 3145732
  29.7 6.6 copy-start.17
  29.7 6.5 collective-permute-start.2
  33.0 5.2 copy-start.33
  36.4 1.9 copy-start.18
  42.0 363.2 %reduce-scatter.6.cloned.1.call-start = ((), (), s32[]{:S(2)}) async-start(), calls=%async_computation.4 | async-start | bytes 2359296 | tf_op jit(solution)/shard_map/reduce_scatter | solution.py:72
  84.2 7.5 collective-permute-start.3
  92.0 46.9 %collective-permute-start.4 = (f32[2048,256]{0,1:T(8,128)S(1)}, f32[2048,256]{0,1:T(8,128)S(1)}, u32[]{:S(2)}, u32[]{:S(2)}) collective-permute-start(f32[2048,256]{0,1:T(8,128)S(1)} %add.75), channel_id=1, source_target_pairs={{0,2},{1,3},{2,0},{3,1},{4,6},{5,7},{6,4},{7,5},{8,10},{9,11},{10,... | collective-permute-start | bytes 6291464 | tf_op jit(solution)/shard_map/ppermute | solution.py:81
  139.2 47.7 %collective-permute-start.5 = (f32[2048,256]{0,1:T(8,128)S(1)}, f32[2048,256]{0,1:T(8,128)S(1)}, u32[]{:S(2)}, u32[]{:S(2)}) collective-permute-start(f32[2048,256]{0,1:T(8,128)S(1)} %add.76), channel_id=1, source_target_pairs={{0,4},{1,5},{2,6},{3,7},{4,0},{5,1},{6,2},{7,3},{8,12},{9,13},{10,... | collective-permute-start | bytes 6291464 | tf_op jit(solution)/shard_map/ppermute | solution.py:81
  186.9 3.4 copy-start.10
  186.9 3.4 copy-start.19
  188.3 1.9 copy-start.5
  192.1 8.4 copy-start.14
  192.1 7.9 copy-start.16
  192.1 7.8 collective-permute-start.6
  193.8 6.7 copy-start.25
  200.0 0.7 copy-start.29
  270.6 18.5 %copy-start.4 = (f32[1,4,256,256]{3,2,1,0:T(8,128)}, f32[1,4,256,256]{3,2,1,0:T(8,128)S(1)}, u32[]{:S(2)}) copy-start(f32[1,4,256,256]{3,2,1,0:T(8,128)S(1)} %multiply_subtract_fusion.2) | copy-start | bytes 3145732
  270.6 7.4 collective-permute-start.7
  280.0 9.1 copy-start.11
  280.0 9.0 collective-permute-start.8
  281.4 7.7 copy-start.27
  289.0 0.7 copy-start.31
  359.5 7.2 collective-permute-start.9
  366.7 1.0 copy-start.20
  373.3 355.7 %reduce-scatter.8.cloned.1.call-start = ((), (), s32[]{:S(2)}) async-start(), calls=%async_computation.5 | async-start | bytes 2359296 | tf_op jit(solution)/shard_map/reduce_scatter | solution.py:72
  408.8 7.5 collective-permute-start.10
  416.6 46.9 %collective-permute-start.11 = (f32[2048,256]{0,1:T(8,128)S(1)}, f32[2048,256]{0,1:T(8,128)S(1)}, u32[]{:S(2)}, u32[]{:S(2)}) collective-permute-start(f32[2048,256]{0,1:T(8,128)S(1)} %add.81), channel_id=1, source_target_pairs={{0,2},{1,3},{2,0},{3,1},{4,6},{5,7},{6,4},{7,5},{8,10},{9,11},{10,... | collective-permute-start | bytes 6291464 | tf_op jit(solution)/shard_map/ppermute | solution.py:81
  463.8 47.9 %collective-permute-start.12 = (f32[2048,256]{0,1:T(8,128)S(1)}, f32[2048,256]{0,1:T(8,128)S(1)}, u32[]{:S(2)}, u32[]{:S(2)}) collective-permute-start(f32[2048,256]{0,1:T(8,128)S(1)} %add.82), channel_id=1, source_target_pairs={{0,4},{1,5},{2,6},{3,7},{4,0},{5,1},{6,2},{7,3},{8,12},{9,13},{10,... | collective-permute-start | bytes 6291464 | tf_op jit(solution)/shard_map/ppermute | solution.py:81
  511.7 3.3 copy-start.21
  513.2 1.9 copy-start.6
  516.9 7.6 copy-start.15
  517.0 7.6 collective-permute-start.13
  518.3 6.2 copy-start.26
  524.5 0.7 copy-start.30
  595.5 18.5 %copy-start.3 = (f32[1,4,256,256]{3,2,1,0:T(8,128)}, f32[1,4,256,256]{3,2,1,0:T(8,128)S(1)}, u32[]{:S(2)}) copy-start(f32[1,4,256,256]{3,2,1,0:T(8,128)S(1)} %multiply_subtract_fusion.1) | copy-start | bytes 3145732
  595.6 7.5 collective-permute-start.14
  605.0 9.1 copy-start.12
  605.0 9.1 collective-permute-start.15
  606.4 7.7 copy-start.28
  614.1 0.7 copy-start.32
  684.1 7.3 copy-start.1
  684.1 7.1 collective-permute-start.16
  691.4 1.9 copy-start.22
  732.6 7.5 collective-permute-start.17
  740.4 46.9 %collective-permute-start.18 = (f32[2048,256]{0,1:T(8,128)S(1)}, f32[2048,256]{0,1:T(8,128)S(1)}, u32[]{:S(2)}, u32[]{:S(2)}) collective-permute-start(f32[2048,256]{0,1:T(8,128)S(1)} %add.88), channel_id=1, source_target_pairs={{0,2},{1,3},{2,0},{3,1},{4,6},{5,7},{6,4},{7,5},{8,10},{9,11},{10,... | collective-permute-start | bytes 6291464 | tf_op jit(solution)/shard_map/ppermute | solution.py:81
  787.7 47.5 %collective-permute-start.19 = (f32[2048,256]{0,1:T(8,128)S(1)}, f32[2048,256]{0,1:T(8,128)S(1)}, u32[]{:S(2)}, u32[]{:S(2)}) collective-permute-start(f32[2048,256]{0,1:T(8,128)S(1)} %add.89), channel_id=1, source_target_pairs={{0,4},{1,5},{2,6},{3,7},{4,0},{5,1},{6,2},{7,3},{8,12},{9,13},{10,... | collective-permute-start | bytes 6291464 | tf_op jit(solution)/shard_map/ppermute | solution.py:81
  835.2 3.3 copy-start.7
  836.6 1.9 copy-start.2
  836.7 1.9 copy-start.23
  840.4 7.6 copy-start.13
  840.4 7.6 collective-permute-start.20
  841.8 6.2 copy-start.24
Sparse Core Ops, SparseCore 0:
  42.1 38.4 reduce-scatter.3
  373.4 31.7 reduce-scatter.5
  697.1 31.8 reduce-scatter.7
